TPU v7x, 32 devices: a whole 2x2x4 slice. The times are simulated.
32 devices in a mesh: dp: 4 (over y, core), px: 2 (over x), py: 4 (over z).
Axes of the slice: x: 2, y: 2, z: 4, core: 2. Of those that a mesh axis runs over, the one named last changes fastest.
Arguments:
- state_a: bfloat16 [4, 16, 128, 128, 128], P('dp', None, 'px', 'py'), may hold values from -6 to 6
- state_b: bfloat16 [4, 16, 128, 128, 128], P('dp', None, 'px', 'py'), may hold values from -6 to 6
- cotan_a: bfloat16 [4, 16, 128, 128, 128], P('dp', None, 'px', 'py'), may hold values from -6 to 6
- cotan_b: bfloat16 [4, 16, 128, 128, 128], P('dp', None, 'px', 'py'), may hold values from -6 to 6
- spectral_weight: bfloat16 [32, 8, 32, 2, 16, 16], P('py', None, 'px'), may hold values from -1 to 1
- point_weight: bfloat16 [16, 16], replicated, may hold values from -1.5 to 1.5
Outputs:
- input_a: bfloat16 [4, 16, 128, 128, 128], P('dp', None, 'px', 'py')
- grad_b: bfloat16 [4, 16, 128, 128, 128], P('dp', None, 'px', 'py')
- spectral_grad: float32 [32, 8, 32, 2, 16, 16], P('py', None, 'px', None, None, 'dp')
- point_grad: float32 [16, 16], replicated
All inputs are finite; a program needn't handle non-finite values.
Results may differ from a plain program's by a relative error of at most 0.0038.
Values sent between devices are 32-bit elements; how exact they have to be, the bound alone decides.
A program may use at most 384 MiB of HBM per device.

v0:
```python
import math

import jax
import jax.numpy as jnp
from jax import lax
from jax.sharding import PartitionSpec as P

NX = 128
NY = 128
NZ = 128
MX = 32
MY = 32
MZ = 8


HIGHEST = lax.Precision.HIGHEST


def kept_frequencies(length_all, length_kept):
    positions = jnp.arange(length_kept, dtype=jnp.int32)
    return jnp.where(positions < length_kept // 2, positions, length_all - length_kept + positions)


def real_table(length_all, length_kept):
    frequency = jnp.arange(length_kept, dtype=jnp.int32)
    positions = jnp.arange(length_all, dtype=jnp.int32)
    phases = frequency[:, None] * positions[None, :] % length_all
    angles = 2.0 * math.pi / length_all * phases.astype(jnp.float32)
    return jnp.stack([jnp.cos(angles), -jnp.sin(angles)])


def complex_table(length_all, length_kept):
    frequency = kept_frequencies(length_all, length_kept)
    positions = jnp.arange(length_all, dtype=jnp.int32)
    phases = positions[:, None] * frequency[None, :] % length_all
    angles = 2.0 * math.pi / length_all * phases.astype(jnp.float32)
    cosine = jnp.cos(angles)
    sine = jnp.sin(angles)
    first = jnp.stack([cosine, -sine], axis=-1)
    second = jnp.stack([sine, cosine], axis=-1)
    return jnp.stack([first, second], axis=1)


def forward_field(field_in, tables):
    x_table, y_table, z_table = tables
    along_x = jnp.einsum("cyzn,rkn->cyzrk", field_in, x_table, precision=HIGHEST)
    along_y = jnp.einsum(
        "cyzrk,yrjt->cjztk",
        lax.all_to_all(along_x, "px", split_axis=4, concat_axis=1, tiled=True),
        y_table,
        precision=HIGHEST,
    )
    return jnp.einsum(
        "cjzrk,zrlt->cjltk",
        lax.all_to_all(along_y, "py", split_axis=1, concat_axis=2, tiled=True),
        z_table,
        precision=HIGHEST,
    )


def inverse_field(spectrum, tables):
    x_table, y_table, z_table = tables
    along_z = jnp.einsum("cjlrk,ztlr->cjztk", spectrum, z_table, precision=HIGHEST)
    along_y = jnp.einsum(
        "cjzrk,ytjr->cyztk",
        lax.all_to_all(along_z, "py", split_axis=2, concat_axis=1, tiled=True),
        y_table,
        precision=HIGHEST,
    )
    return jnp.einsum(
        "cyzrk,rkn->cyzn",
        lax.all_to_all(along_y, "px", split_axis=1, concat_axis=4, tiled=True),
        x_table,
        precision=HIGHEST,
    )


def spectral_product(spectrum, weight):
    pattern = "cjlk,jlkcd->djlk"
    real_in = spectrum[:, :, :, 0]
    imag_in = spectrum[:, :, :, 1]
    w_real = weight[:, :, :, 0]
    w_imag = weight[:, :, :, 1]
    out_real = jnp.einsum(pattern, real_in, w_real, precision=HIGHEST) - jnp.einsum(
        pattern, imag_in, w_imag, precision=HIGHEST
    )
    out_imag = jnp.einsum(pattern, real_in, w_imag, precision=HIGHEST) + jnp.einsum(
        pattern, imag_in, w_real, precision=HIGHEST
    )
    return jnp.stack([out_real, out_imag], axis=3)


def spectral_adjoint(back_spec, weight):
    pattern = "djlk,jlkcd->cjlk"
    real_in = back_spec[:, :, :, 0]
    imag_in = back_spec[:, :, :, 1]
    w_real = weight[:, :, :, 0]
    w_imag = weight[:, :, :, 1]
    out_real = jnp.einsum(pattern, real_in, w_real, precision=HIGHEST) + jnp.einsum(
        pattern, imag_in, w_imag, precision=HIGHEST
    )
    out_imag = jnp.einsum(pattern, imag_in, w_real, precision=HIGHEST) - jnp.einsum(
        pattern, real_in, w_imag, precision=HIGHEST
    )
    return jnp.stack([out_real, out_imag], axis=3)


def spectral_outer(spectrum, back_spec):
    pattern = "cjlk,djlk->jlkcd"
    spec_real = spectrum[:, :, :, 0]
    spec_imag = spectrum[:, :, :, 1]
    back_real = back_spec[:, :, :, 0]
    back_imag = back_spec[:, :, :, 1]
    grad_real = jnp.einsum(pattern, spec_real, back_real, precision=HIGHEST) + jnp.einsum(
        pattern, spec_imag, back_imag, precision=HIGHEST
    )
    grad_imag = jnp.einsum(pattern, spec_real, back_imag, precision=HIGHEST) - jnp.einsum(
        pattern, spec_imag, back_real, precision=HIGHEST
    )
    return jnp.stack([grad_real, grad_imag], axis=3)


def per_device(state_a, state_b, cotan_a, cotan_b, spectral_weight, point_weight):
    tables = (real_table(NX, MX), complex_table(NY, MY), complex_table(NZ, MZ))
    samples = lax.axis_size("dp")
    scale_f = 1.0 / math.sqrt(NX * NY * NZ)
    scale_i = 1.0 / math.sqrt(MX * MY * MZ)
    grad_scale = math.sqrt(MX * MY * MZ / (samples * NX * NY * NZ))
    point_scale = 1.0 / math.sqrt(samples * NX * NY * NZ)
    weight = spectral_weight.astype(jnp.float32)
    field_b = state_b[0]
    spectrum = forward_field(field_b.astype(jnp.float32), tables) * scale_f
    mixed_spec = spectral_product(spectrum, weight)
    local_point = jnp.einsum(
        "cyzn,cd->dyzn", field_b, point_weight, preferred_element_type=jnp.float32
    )
    hidden = inverse_field(mixed_spec, tables) * scale_i + local_point
    activated, pullback = jax.vjp(jax.nn.gelu, hidden)
    input_a = (state_a[0].astype(jnp.float32) - activated).astype(jnp.bfloat16)
    slope_grad = pullback(cotan_a[0].astype(jnp.float32))[0].astype(jnp.bfloat16)
    back_spec = forward_field(slope_grad.astype(jnp.float32), tables) * scale_i
    spec_grad = spectral_adjoint(back_spec, weight)
    point_back = jnp.einsum(
        "dyzn,cd->cyzn", slope_grad, point_weight, preferred_element_type=jnp.float32
    )
    point_local = jnp.einsum(
        "cyzn,dyzn->cd", field_b, slope_grad, preferred_element_type=jnp.float32
    )
    point_total = lax.psum(point_local, ("dp", "px", "py")) * point_scale
    second = (
        cotan_b[0].astype(jnp.float32) + inverse_field(spec_grad, tables) * scale_f + point_back
    )
    grad_b = second.astype(jnp.bfloat16)
    grad_local = spectral_outer(spectrum, back_spec) * grad_scale
    spectral_grad = lax.psum_scatter(grad_local, "dp", scatter_dimension=5, tiled=True)
    return (input_a[None], grad_b[None], spectral_grad, point_total)


def solution(mesh):
    return jax.shard_map(
        per_device,
        mesh=mesh,
        in_specs=(
            P("dp", None, "px", "py", None),
            P("dp", None, "px", "py", None),
            P("dp", None, "px", "py", None),
            P("dp", None, "px", "py", None),
            P("py", None, "px", None, None, None),
            P(),
        ),
        out_specs=(
            P("dp", None, "px", "py", None),
            P("dp", None, "px", "py", None),
            P("py", None, "px", None, None, "dp"),
            P(),
        ),
        check_vma=False,
    )
```

profile of v0, /device:TPU:0, one launch (start us, length us, event | category | flops | bytes accessed | tf_op | source)
XLA Modules:
  0.0 1877.6 jit_solution(11953097261368654046)
XLA Ops:
  81.5 93.6 %all-to-all-done = f32[2,1,1048576]{2,1,0:T(1,128)} async-done(((f32[2,1,1048576]{2,1,0:T(1,128)}), f32[2,1,1048576]{2,1,0:T(1,128)}, u32[]{:S(2)}, u32[]{:S(2)}) %all-to-all-start) | async-done | bytes 8388640 | tf_op jit(solution)/shard_map/all_to_all | solution.py:49
  175.7 33.2 %reduce.16 = f32[2,1048576]{1,0:T(2,128)} reduce(f32[2,1,1048576]{2,1,0:T(1,128)} %all-to-all-done, f32[]{:T(128)} %broadcast.467), dimensions={1}, to_apply=%all_to_all.104.reduce_sub_computation | reduce | bytes 16777220 | tf_op jit(solution)/shard_map/all_to_all | solution.py:49
  318.9 46.9 %all-to-all-done.1 = f32[4,1,131072]{2,1,0:T(1,128)} async-done(((f32[4,1,131072]{2,1,0:T(1,128)}), f32[4,1,131072]{2,1,0:T(1,128)}, u32[]{:S(2)}, u32[]{:S(2)}) %all-to-all-start.1) | async-done | bytes 2097184 | tf_op jit(solution)/shard_map/all_to_all | solution.py:55
  448.7 51.3 %all_to_all.144 = f32[4,1,131072]{2,1,0:T(1,128)} all-to-all(f32[4,1,131072]{2,1,0:T(1,128)S(1)} %reshape.404), channel_id=1, replica_groups=mesh['dp'=4,'px'=2,'py'=4] {'py'}, dimensions={0} | all-to-all | bytes 4194304 | tf_op jit(solution)/shard_map/all_to_all | solution.py:66
  590.0 30.2 %reshape.406 = f32[2,1,1048576]{2,1,0:T(1,128)} reshape(f32[128,2,16,16,32]{4,3,2,1,0:T(8,128)} %bitcast.323) | data formatting | bytes 16777216
  639.7 79.0 %all-to-all-done.3 = f32[2,1,1048576]{2,1,0:T(1,128)} async-done(((f32[2,1,1048576]{2,1,0:T(1,128)}), f32[2,1,1048576]{2,1,0:T(1,128)}, u32[]{:S(2)}, u32[]{:S(2)}) %all-to-all-start.3) | async-done | bytes 8388640 | tf_op jit(solution)/shard_map/all_to_all | solution.py:72
  718.6 33.2 %reduce.19 = f32[2,1048576]{1,0:T(2,128)} reduce(f32[2,1,1048576]{2,1,0:T(1,128)} %all-to-all-done.3, f32[]{:T(128)} %broadcast.467), dimensions={1}, to_apply=%all_to_all.116.reduce_sub_computation | reduce | bytes 16777220 | tf_op jit(solution)/shard_map/all_to_all | solution.py:72
  751.8 33.7 %reshape.407 = f32[128,2,16,16,32]{4,3,2,1,0:T(8,128)} reshape(f32[2,1048576]{1,0:T(2,128)} %reduce.19) | data formatting | bytes 16777216
  785.5 35.9 %copy.230 = f32[16,2,64,32,2,16]{2,1,5,4,3,0:T(2,128)} copy(f32[16,2,64,32,2,16]{3,5,0,4,2,1:T(8,128)} %bitcast.324) | data formatting | bytes 16777216 | tf_op jit(solution)/shard_map/all_to_all | solution.py:72
  834.2 30.4 %copy.123 = f32[16,64,32,2,32]{4,2,3,1,0:T(8,128)} copy(f32[16,64,32,2,32]{1,4,3,2,0:T(8,128)} %bitcast.328) | data formatting | bytes 16777216 | tf_op jit(solution)/shard_map/all_to_all | solution.py:72
  864.6 49.9 %fusion.2 = (bf16[16,64,32,128]{3,2,1,0:T(8,128)(2,1)}, bf16[1,16,64,32,128]{4,3,2,1,0:T(8,128)(2,1)}) fusion(bf16[1,16,64,32,128]{4,3,2,1,0:T(8,128)(2,1)} %param.8, bf16[1,16,64,32,128]{4,3,2,1,0:T(8,128)(2,1)} %param.6, f32[16,64,32,128]{3,0,2,1:T(8,128)} %fusion.37, f32[16,64,32,2,32]{4,2,3,1,0:T(8,128)} %copy.123, f32[2,32,128,1,1]{2,1,0,4,3:T(8,128)S(1)} %fusion.132), kind=kOutput, calls=%fused_computation.6 | convolution fusion | flops 3334471680 | bytes 58753024 | tf_op jit(solution)/shard_map/cyzrk,rkn->cyzn/dot_general | solution.py:70
  936.2 29.1 %copy.127 = f32[16,64,32,2,32]{1,2,3,0,4:T(8,128)} copy(f32[16,64,32,2,32]{4,2,3,1,0:T(8,128)} %fusion.22) | data formatting | bytes 16777216 | tf_op jit(solution)/shard_map/cyzn,rkn->cyzrk/dot_general | solution.py:46
  986.8 101.5 %all_to_all.145 = f32[2,1,1048576]{2,1,0:T(1,128)} all-to-all(f32[2,1,1048576]{2,1,0:T(1,128)} %reshape.408), channel_id=1, replica_groups=mesh['dp'=4,'px'=2,'py'=4] {'px'}, dimensions={0} | all-to-all | bytes 16777216 | tf_op jit(solution)/shard_map/all_to_all | solution.py:49
  1088.3 32.8 %reduce.20 = f32[2,1048576]{1,0:T(2,128)} reduce(f32[2,1,1048576]{2,1,0:T(1,128)} %all_to_all.145, f32[]{:T(128)} %broadcast.467), dimensions={1}, to_apply=%all_to_all.120.reduce_sub_computation | reduce | bytes 16777220 | tf_op jit(solution)/shard_map/all_to_all | solution.py:49
  1142.3 29.0 %copy.129 = f32[16,2,64,32,2,16]{2,1,3,4,5,0:T(2,128)} copy(f32[16,2,64,32,2,16]{2,3,4,0,5,1:T(8,128)} %bitcast.339) | data formatting | bytes 16777216 | tf_op jit(solution)/shard_map/all_to_all | solution.py:49
  1224.6 50.0 %all_to_all.146 = f32[4,1,131072]{2,1,0:T(1,128)} all-to-all(f32[4,1,131072]{2,1,0:T(1,128)S(1)} %reshape.410), channel_id=1, replica_groups=mesh['dp'=4,'px'=2,'py'=4] {'py'}, dimensions={0} | all-to-all | bytes 4194304 | tf_op jit(solution)/shard_map/all_to_all | solution.py:55
  1375.1 35.1 %all-to-all-done.6 = f32[4,1,131072]{2,1,0:T(1,128)} async-done(((f32[4,1,131072]{2,1,0:T(1,128)}), f32[4,1,131072]{2,1,0:T(1,128)}, u32[]{:S(2)}, u32[]{:S(2)}) %all-to-all-start.6) | async-done | bytes 2097184 | tf_op jit(solution)/shard_map/all_to_all | solution.py:66
  1500.9 30.2 %reshape.414 = f32[2,1,1048576]{2,1,0:T(1,128)} reshape(f32[128,2,16,16,32]{4,3,2,1,0:T(8,128)} %bitcast.325) | data formatting | bytes 16777216
  1553.4 109.0 %psum.7 = f32[16,16]{0,1:T(8,128)S(1)} all-reduce(f32[16,16]{0,1:T(8,128)S(1)} %fusion.53), channel_id=1, replica_groups=mesh['dp'=4,'px'=2,'py'=4] {'dp','px','py'}, use_global_device_ids=true, to_apply=%region_1.2 | all-reduce | flops 256 | bytes 2048 | tf_op jit(solution)/shard_map/psum | solution.py:149
  1685.4 33.0 %reduce.23 = f32[2,1048576]{1,0:T(2,128)} reduce(f32[2,1,1048576]{2,1,0:T(1,128)} %all-to-all-done.7, f32[]{:T(128)} %broadcast.467), dimensions={1}, to_apply=%all_to_all.132.reduce_sub_computation | reduce | bytes 16777220 | tf_op jit(solution)/shard_map/all_to_all | solution.py:72
  1718.4 33.9 %reshape.415 = f32[128,2,16,16,32]{4,3,2,1,0:T(8,128)} reshape(f32[2,1048576]{1,0:T(2,128)} %reduce.23) | data formatting | bytes 16777216
  1752.3 35.9 %copy.238 = f32[16,2,64,32,2,16]{2,1,5,4,3,0:T(2,128)} copy(f32[16,2,64,32,2,16]{3,5,0,4,2,1:T(8,128)} %bitcast.326) | data formatting | bytes 16777216 | tf_op jit(solution)/shard_map/all_to_all | solution.py:72
  1801.0 30.5 %copy.141 = f32[16,64,32,2,32]{4,2,3,1,0:T(8,128)} copy(f32[16,64,32,2,32]{1,4,3,2,0:T(8,128)} %bitcast.331) | data formatting | bytes 16777216 | tf_op jit(solution)/shard_map/all_to_all | solution.py:72
  1831.4 39.2 %fusion.42 = bf16[1,16,64,32,128]{4,3,2,1,0:T(8,128)(2,1)} fusion(f32[64,32,128,16]{2,3,1,0:T(8,128)} %fusion.34, f32[16,64,32,2,32]{4,2,3,1,0:T(8,128)} %copy.141, bf16[1,16,64,32,128]{4,3,2,1,0:T(8,128)(2,1)} %param.9, f32[1,32,128]{2,1,0:T(8,128)S(1)} %copy-done.11, f32[1,32,128]{2,1,0:T(8,128)S(1)} %copy-done.14), kind=kOutput, calls=%fused_computation.62 | convolution fusion | flops 3242205184 | bytes 41975808 | tf_op jit(solution)/shard_map/cyzrk,rkn->cyzn/dot_general | solution.py:70
  (132 shorter events, 756.5 us)
Async XLA Ops:
  7.2 620.1 %copy-start = (bf16[16,16]{1,0:T(8,128)(2,1)S(1)}, bf16[16,16]{1,0:T(8,128)(2,1)}, u32[]{:S(2)}) copy-start(bf16[16,16]{1,0:T(8,128)(2,1)} %param.11) | copy-start | bytes 1540
  7.3 26.5 %copy-start.9 = (f32[1,32,128]{2,1,0:T(8,128)}, f32[1,32,128]{2,1,0:T(8,128)S(1)}, u32[]{:S(2)}) copy-start(f32[1,32,128]{2,1,0:T(8,128)S(1)} %get-tuple-element.50) | copy-start | bytes 49156
  7.3 26.5 %copy-start.12 = (f32[1,32,128]{2,1,0:T(8,128)}, f32[1,32,128]{2,1,0:T(8,128)S(1)}, u32[]{:S(2)}) copy-start(f32[1,32,128]{2,1,0:T(8,128)S(1)} %get-tuple-element.51) | copy-start | bytes 49156
  74.4 100.8 %all-to-all-start = ((f32[2,1,1048576]{2,1,0:T(1,128)}), f32[2,1,1048576]{2,1,0:T(1,128)}, u32[]{:S(2)}, u32[]{:S(2)}) async-start(f32[2,1,1048576]{2,1,0:T(1,128)} %reshape.400), calls=%async_computation | async-start | bytes 16777216 | tf_op jit(solution)/shard_map/all_to_all | solution.py:49
  81.5 471.1 %copy-start.5 = (f32[128,1,32,2]{0,2,1,3:T(8,128)}, f32[128,1,32,2]{0,2,1,3:T(8,128)S(1)}, u32[]{:S(2)}) copy-start(f32[128,1,32,2]{0,2,1,3:T(8,128)S(1)} %get-tuple-element.40) | copy-start | bytes 98308
  81.5 471.1 %copy-start.7 = (f32[128,1,32,2]{0,2,1,3:T(8,128)}, f32[128,1,32,2]{0,2,1,3:T(8,128)S(1)}, u32[]{:S(2)}) copy-start(f32[128,1,32,2]{0,2,1,3:T(8,128)S(1)} %get-tuple-element.41) | copy-start | bytes 98308
  313.3 52.5 %all-to-all-start.1 = ((f32[4,1,131072]{2,1,0:T(1,128)}), f32[4,1,131072]{2,1,0:T(1,128)}, u32[]{:S(2)}, u32[]{:S(2)}) async-start(f32[4,1,131072]{2,1,0:T(1,128)} %reshape.402), calls=%async_computation.1 | async-start | bytes 4194304 | tf_op jit(solution)/shard_map/all_to_all | solution.py:55
  318.9 105.3 %copy-start.15 = (f32[128,1,8,2]{0,2,1,3:T(8,128)}, f32[128,1,8,2]{0,2,1,3:T(8,128)S(1)}, u32[]{:S(2)}) copy-start(f32[128,1,8,2]{0,2,1,3:T(8,128)S(1)} %get-tuple-element.42) | copy-start | bytes 24580
  318.9 105.3 %copy-start.17 = (f32[128,1,8,2]{0,2,1,3:T(8,128)}, f32[128,1,8,2]{0,2,1,3:T(8,128)S(1)}, u32[]{:S(2)}) copy-start(f32[128,1,8,2]{0,2,1,3:T(8,128)S(1)} %get-tuple-element.43) | copy-start | bytes 24580
  406.5 16.5 copy-start.1
  406.9 16.2 copy-start.3
  620.2 7.1 copy-start.10
  620.2 7.1 copy-start.13
  620.2 98.4 %all-to-all-start.3 = ((f32[2,1,1048576]{2,1,0:T(1,128)}), f32[2,1,1048576]{2,1,0:T(1,128)}, u32[]{:S(2)}, u32[]{:S(2)}) async-start(f32[2,1,1048576]{2,1,0:T(1,128)} %reshape.406), calls=%async_computation.3 | async-start | bytes 16777216 | tf_op jit(solution)/shard_map/all_to_all | solution.py:72
  1171.3 16.4 copy-start.6
  1171.3 16.4 copy-start.8
  1300.6 6.6 copy-start.18
  1348.9 14.7 copy-start.2
  1348.9 14.7 copy-start.4
  1359.1 51.1 %all-to-all-start.6 = ((f32[4,1,131072]{2,1,0:T(1,128)}), f32[4,1,131072]{2,1,0:T(1,128)}, u32[]{:S(2)}, u32[]{:S(2)}) async-start(f32[4,1,131072]{2,1,0:T(1,128)} %reshape.412), calls=%async_computation.6 | async-start | bytes 4194304 | tf_op jit(solution)/shard_map/all_to_all | solution.py:66
  1363.6 313.6 %reduce-scatter.2.cloned.1.call-start = ((), (), s32[]{:S(2)}) async-start(), calls=%async_computation.9 | async-start | bytes 20971520 | tf_op jit(solution)/shard_map/reduce_scatter | solution.py:155
  1531.0 154.4 %all-to-all-start.7 = ((f32[2,1,1048576]{2,1,0:T(1,128)}), f32[2,1,1048576]{2,1,0:T(1,128)}, u32[]{:S(2)}, u32[]{:S(2)}) async-start(f32[2,1,1048576]{2,1,0:T(1,128)} %reshape.414), calls=%async_computation.7 | async-start | bytes 16777216 | tf_op jit(solution)/shard_map/all_to_all | solution.py:72
  1801.0 30.5 %copy-start.11 = (f32[1,32,128]{2,1,0:T(8,128)S(1)}, f32[1,32,128]{2,1,0:T(8,128)}, u32[]{:S(2)}) copy-start(f32[1,32,128]{2,1,0:T(8,128)} %copy-done.9) | copy-start | bytes 49156
  1801.0 30.5 %copy-start.14 = (f32[1,32,128]{2,1,0:T(8,128)S(1)}, f32[1,32,128]{2,1,0:T(8,128)}, u32[]{:S(2)}) copy-start(f32[1,32,128]{2,1,0:T(8,128)} %copy-done.12) | copy-start | bytes 49156
  (1 other events, 6.6 us)
Sparse Core Ops, SparseCore 0:
  1375.2 126.5 reduce-scatter.1
where the time goes:
time: 1890 us; the launch traced here: 1880 us
  local copies, waits for them, and re-layouts  798 us (42%)
  blocking collectives  312 us (17%)
  matrix products  265 us (14%)
  waiting for transfers between devices  255 us (13%)
  other arithmetic  202 us (11%)
  starting transfers between devices  31.2 us (2%)
    unnamed x62, local copies, waits for them, and re-layouts  292 us
    all_to_all x6, local copies, waits for them, and re-layouts, inverse_field(): lax.all_to_all(along_y, 'px', split_axis=1, concat_axis=4, tiled=True)  158 us
    psum x1, blocking collectives, per_device(): point_total = lax.psum(point_local, ('dp', 'px', 'py')) * point_scale  109 us
    all_to_all x1, blocking collectives, forward_field(): lax.all_to_all(along_x, 'px', split_axis=4, concat_axis=1, tiled=True)  101 us
    all_to_all x1, waiting for transfers between devices, forward_field(): lax.all_to_all(along_x, 'px', split_axis=4, concat_axis=1, tiled=True)  93.6 us
    all_to_all x5, local copies, waits for them, and re-layouts, forward_field(): lax.all_to_all(along_x, 'px', split_axis=4, concat_axis=1, tiled=True)  91 us
    dot_general x2, matrix products, inverse_field(): jnp.einsum('cyzrk,rkn->cyzn', lax.all_to_all(along_y, 'px', split_axis=1,...  89.1 us
    all_to_all x2, waiting for transfers between devices, inverse_field(): lax.all_to_all(along_y, 'px', split_axis=1, concat_axis=4, tiled=True)  79 us
  transfers between devices with their start and end apart: 6, of which 4 were waited for; matrix products, arithmetic and copies ran while one was open for 10% of the time, Pallas kernels for 0%

commit v1 on v0

v1 whole, which is shorter than its diff:
```python
import math

import jax
import jax.numpy as jnp
import numpy as np
from jax import lax
from jax.experimental import pallas as pl
from jax.experimental.pallas import tpu as pltpu
from jax.sharding import PartitionSpec as P

MX = 32
MY = 32
MZ = 8
GROUP = 4
SUB = 16
LIMIT = 56 * 1024 * 1024
INTERPRET = False
F32 = jnp.float32
BF16 = jnp.bfloat16


def kept(length_all, length_kept, position):
    return jnp.where(position < length_kept // 2, position, length_all - length_kept + position)


def angle(product, length_all):
    return (product % length_all).astype(F32) * (2.0 * math.pi / length_all)


def split(value):
    high = lax.reduce_precision(value, 8, 7)
    return high.astype(BF16), (value - high).astype(BF16)


def synthesis_table(shape):
    ys, zs, ny, nz = shape
    mode = lax.broadcasted_iota(jnp.int32, (1, MY * MZ), 1)
    fy = kept(ny, MY, mode // MZ)
    fz = kept(nz, MZ, mode % MZ)
    y = lax.axis_index("px") * ys + lax.broadcasted_iota(jnp.int32, (ys, 1), 0)
    z = lax.axis_index("py") * zs + lax.broadcasted_iota(jnp.int32, (zs, 1), 0)
    ay = angle(fy * y, ny)
    az = angle(fz * z, nz)
    cy, sy = jnp.cos(ay)[:, None, :], jnp.sin(ay)[:, None, :]
    cz, sz = jnp.cos(az)[None], jnp.sin(az)[None]
    table = jnp.concatenate([cy * cz - sy * sz, -(sy * cz + cy * sz)], axis=2)
    return table.reshape(ys * zs, 2 * MY * MZ)


def analysis_table(shape):
    ys, zs, ny, nz = shape
    cell = lax.broadcasted_iota(jnp.int32, (1, ys * zs), 1)
    y = lax.axis_index("px") * ys + cell // zs
    z = lax.axis_index("py") * zs + cell % zs
    fy = kept(ny, MY, lax.broadcasted_iota(jnp.int32, (MY, 1), 0))
    fz = kept(nz, MZ, lax.broadcasted_iota(jnp.int32, (MZ, 1), 0))
    ay = angle(fy * y, ny)
    az = angle(fz * z, nz)
    cy, sy = jnp.cos(ay)[:, None, :], jnp.sin(ay)[:, None, :]
    cz, sz = jnp.cos(az)[None], jnp.sin(az)[None]
    table = jnp.stack([cy * cz - sy * sz, -(sy * cz + cy * sz)])
    return table.reshape(2 * MY * MZ, ys * zs)


def x_tables(px, nx):
    kk = MX // px
    k = np.arange(MX).reshape(px, kk)
    phase = 2.0 * np.pi / nx * (k[:, :, None] * np.arange(nx) % nx)
    cosine, sine = np.cos(phase), np.sin(phase)
    table = np.zeros((2, px, GROUP, 2, kk, GROUP, nx))
    for c in range(GROUP):
        table[0, :, c, 0, :, c] = cosine
        table[0, :, c, 1, :, c] = -sine
        table[1, :, c, 0, :, c] = sine
        table[1, :, c, 1, :, c] = cosine
    table = table.reshape(2, 2 * MX * GROUP, GROUP * nx)
    high = table.astype(BF16)
    low = (table - high.astype(np.float64)).astype(BF16)
    return high, low


def dot(a, b):
    return jnp.dot(a, b, preferred_element_type=F32)


def cut(value):
    high = value.astype(BF16)
    return high, (value - high.astype(F32)).astype(BF16)


def dot3(a, high, low):
    ahigh, alow = cut(a)
    return dot(ahigh, high) + dot(alow, high) + dot(ahigh, low)


def to_modes(b0, b1, xh_ref, xl_ref):
    return dot3(b0, xh_ref[0], xl_ref[0]) + dot3(b1, xh_ref[1], xl_ref[1])


def store_modes(out_ref, group, value, px, py):
    wide = value.shape[1] // px
    tall = value.shape[0] // py
    for i in range(px):
        for j in range(py):
            out_ref[i * py + j, group] = value[j * tall : (j + 1) * tall, i * wide : (i + 1) * wide]


def build_fields(spec_ref, xh_ref, xl_ref, gh_ref, gl_ref, px, py):
    modes = MY * MZ
    for g in range(spec_ref.shape[1]):
        rows = []
        for j in range(py):
            rows.append(jnp.concatenate([spec_ref[i * py + j, g] for i in range(px)], axis=1))
        value = jnp.concatenate(rows, axis=0)
        for t in range(2):
            high, low = cut(dot3(value, xh_ref[t], xl_ref[t]))
            half = high.shape[1] // 2
            for h in range(2):
                gh_ref[2 * g + h, t * modes : (t + 1) * modes] = high[:, h * half : (h + 1) * half]
                gl_ref[2 * g + h, t * modes : (t + 1) * modes] = low[:, h * half : (h + 1) * half]


def pair_of(ref, start):
    chans, _, nx = ref.shape
    first = ref[:, pl.ds(start, SUB), :].reshape(chans * SUB, nx)
    second = ref[:, pl.ds(start + SUB, SUB), :].reshape(chans * SUB, nx)
    return jnp.concatenate([first, second], axis=1)


def channel_mix(kron_ref, in_ref, out_ref):
    chans, rows, nx = in_ref.shape

    def body(q, carry):
        start = pl.multiple_of(q * 2 * SUB, 2 * SUB)
        value = dot(kron_ref[...], pair_of(in_ref, start))
        out_ref[:, pl.ds(start, SUB), :] = value[:, :nx].reshape(chans, SUB, nx)
        out_ref[:, pl.ds(start + SUB, SUB), :] = value[:, nx:].reshape(chans, SUB, nx)
        return carry

    lax.fori_loop(0, rows // (2 * SUB), body, 0)


def forward_kernel(px, py, v_ref, th_ref, tl_ref, xh_ref, xl_ref, out_ref):
    modes = MY * MZ
    parts = []
    for p in range(GROUP // 2):
        value = jnp.concatenate([v_ref[2 * p], v_ref[2 * p + 1]], axis=1)
        parts.append(dot(th_ref[...], value) + dot(tl_ref[...], value))
    b0 = jnp.concatenate([part[:modes] for part in parts], axis=1)
    b1 = jnp.concatenate([part[modes:] for part in parts], axis=1)
    store_modes(out_ref, 0, to_modes(b0, b1, xh_ref, xl_ref), px, py)


def middle_kernel(
    px, py, steps, spec_ref, vb_ref, va_ref, ca_ref, uh_ref, ul_ref, th_ref, tl_ref, xh_ref, xl_ref, fh_ref, fl_ref,
    kron_ref, ia_ref, sl_ref, back_ref, point_ref, gh_ref, gl_ref, acc_ref, mix_ref,
):
    step = pl.program_id(0)
    modes = MY * MZ
    nx = vb_ref.shape[2]
    chans, rows = vb_ref.shape[:2]

    @pl.when(step == 0)
    def _():
        build_fields(spec_ref, xh_ref, xl_ref, gh_ref, gl_ref, px, py)
        acc_ref[...] = jnp.zeros_like(acc_ref)
        point_ref[...] = jnp.zeros_like(point_ref)

    channel_mix(kron_ref, vb_ref, mix_ref)
    c0 = math.sqrt(2.0 / math.pi)

    def body(p, carry):
        field = dot(uh_ref[...], gh_ref[p]) + dot(ul_ref[...], gh_ref[p]) + dot(uh_ref[...], gl_ref[p])
        slopes = []
        for h in range(2):
            d = 2 * p + h
            v = field[:, h * nx : (h + 1) * nx] + mix_ref[d]
            v2 = v * v
            t = jnp.tanh(v * (c0 + (c0 * 0.044715) * v2))
            half = 0.5 + 0.5 * t
            ia_ref[d] = (va_ref[d].astype(F32) - v * half).astype(BF16)
            deriv = half + (0.5 * v) * (1.0 - t * t) * (c0 + (3.0 * c0 * 0.044715) * v2)
            slope = (ca_ref[d].astype(F32) * deriv).astype(BF16)
            sl_ref[d] = slope
            slopes.append(slope)
        both = jnp.concatenate(slopes, axis=1)
        acc_ref[p] += dot(th_ref[...], both) + dot(tl_ref[...], both)
        return carry

    lax.fori_loop(0, chans // 2, body, 0)

    def point_body(q, carry):
        start = pl.multiple_of(q * 2 * SUB, 2 * SUB)
        point_ref[...] += lax.dot_general(
            pair_of(vb_ref, start), pair_of(sl_ref, start), (((1,), (1,)), ((), ())), preferred_element_type=F32
        )
        return carry

    lax.fori_loop(0, rows // (2 * SUB), point_body, 0)

    @pl.when(step == steps - 1)
    def _():
        for g in range(chans // GROUP):
            parts = [acc_ref[2 * g + h] for h in range(2)]
            b0 = jnp.concatenate([part[:modes] for part in parts], axis=1)
            b1 = jnp.concatenate([part[modes:] for part in parts], axis=1)
            store_modes(back_ref, g, to_modes(b0, b1, fh_ref, fl_ref), px, py)


def last_kernel(
    px, py, spec_ref, sl_ref, cb_ref, uh_ref, ul_ref, xh_ref, xl_ref, kron_ref, out_ref, gh_ref, gl_ref, mix_ref
):
    nx = sl_ref.shape[2]

    @pl.when(pl.program_id(0) == 0)
    def _():
        build_fields(spec_ref, xh_ref, xl_ref, gh_ref, gl_ref, px, py)

    channel_mix(kron_ref, sl_ref, mix_ref)

    def body(p, carry):
        field = dot(uh_ref[...], gh_ref[p]) + dot(ul_ref[...], gh_ref[p]) + dot(uh_ref[...], gl_ref[p])
        for h in range(2):
            d = 2 * p + h
            value = cb_ref[d].astype(F32) + field[:, h * nx : (h + 1) * nx] + mix_ref[d]
            out_ref[d] = value.astype(BF16)
        return carry

    lax.fori_loop(0, sl_ref.shape[0] // 2, body, 0)


def whole(shape):
    return pl.BlockSpec(shape, lambda i: (0,) * len(shape), pipeline_mode=pl.Buffered(1))


def per_device(state_a, state_b, cotan_a, cotan_b, spectral_weight, point_weight):
    samples, px, py = (lax.axis_size(name) for name in ("dp", "px", "py"))
    _, chans, ys, zs, nx = state_b.shape
    ny, nz = ys * px, zs * py
    cells, modes = ys * zs, MY * MZ
    groups = chans // GROUP
    kk = MX // px
    tall, wide = modes // py, 2 * MX * GROUP // px
    own = tall * kk
    scale_f = 1.0 / math.sqrt(nx * ny * nz)
    scale_i = 1.0 / math.sqrt(MX * MY * MZ)
    grad_scale = math.sqrt(MX * MY * MZ / (samples * nx * ny * nz))
    point_scale = 1.0 / math.sqrt(samples * nx * ny * nz)
    shape = (ys, zs, ny, nz)
    th, tl = split(analysis_table(shape))
    uh, ul = split(synthesis_table(shape))
    xh, xl = x_tables(px, nx)
    fh, fl = (jnp.asarray(np.ascontiguousarray(table.transpose(0, 2, 1))) for table in (xh, xl))
    xh, xl = jnp.asarray(xh), jnp.asarray(xl)
    eye = jnp.eye(SUB, dtype=BF16)
    kron_f = (point_weight.T[:, None, :, None] * eye[None, :, None, :]).reshape(chans * SUB, chans * SUB)
    kron_b = (point_weight[:, None, :, None] * eye[None, :, None, :]).reshape(chans * SUB, chans * SUB)
    field_a, field_b, cot_a, cot_b = (
        value.reshape(chans, cells, nx) for value in (state_a, state_b, cotan_a, cotan_b)
    )
    part_shape = jax.ShapeDtypeStruct((px * py, groups, tall, wide), F32)
    params = pltpu.CompilerParams(vmem_limit_bytes=LIMIT)

    part = pl.pallas_call(
        lambda *refs: forward_kernel(px, py, *refs),
        grid=(groups,),
        in_specs=[
            pl.BlockSpec((GROUP, cells, nx), lambda i: (i, 0, 0)),
            whole(th.shape), whole(tl.shape), whole(fh.shape), whole(fl.shape),
        ],
        out_specs=pl.BlockSpec((px * py, 1, tall, wide), lambda i: (0, i, 0, 0)),
        out_shape=part_shape,
        compiler_params=params,
        interpret=INTERPRET,
        name="forward",
    )(field_b, th, tl, fh, fl)

    def scatter(value):
        value = lax.psum_scatter(value, ("px", "py"), scatter_dimension=0, tiled=True)
        value = value.reshape(groups, tall, GROUP, 2, kk).transpose(3, 0, 2, 1, 4)
        return value.reshape(2, chans, own)

    def gather(real, imag):
        value = jnp.stack([real, imag]).reshape(2, groups, GROUP, tall, kk).transpose(1, 3, 2, 0, 4)
        value = value.reshape(1, groups, tall, wide)
        return lax.all_gather(value, ("px", "py"), axis=0, tiled=True)

    weight = spectral_weight.transpose(3, 4, 5, 0, 1, 2).reshape(2, chans, chans, own).astype(F32)
    w_real, w_imag = weight[0], weight[1]
    spectrum = scatter(part) * scale_f
    s_real, s_imag = spectrum[0][:, None], spectrum[1][:, None]
    mixed = gather(
        jnp.sum(s_real * w_real - s_imag * w_imag, axis=0) * scale_i,
        jnp.sum(s_real * w_imag + s_imag * w_real, axis=0) * scale_i,
    )

    rows = min(256, cells)
    steps = cells // rows
    block = pl.BlockSpec((chans, rows, nx), lambda i: (0, i, 0))
    u_block = pl.BlockSpec((rows, 2 * modes), lambda i: (i, 0))
    t_block = pl.BlockSpec((2 * modes, rows), lambda i: (0, i))
    field_shape = jax.ShapeDtypeStruct((chans, cells, nx), BF16)
    side = chans * SUB
    g_scratch = [pltpu.VMEM((chans // 2, 2 * modes, 2 * nx), BF16)] * 2
    input_a, slope, back_part, point = pl.pallas_call(
        lambda *refs: middle_kernel(px, py, steps, *refs),
        grid=(steps,),
        in_specs=[
            whole(part_shape.shape), block, block, block, u_block, u_block, t_block, t_block,
            whole(xh.shape), whole(xl.shape), whole(fh.shape), whole(fl.shape), whole((side, side)),
        ],
        out_specs=[block, block, whole(part_shape.shape), whole((side, side))],
        out_shape=[field_shape, field_shape, part_shape, jax.ShapeDtypeStruct((side, side), F32)],
        scratch_shapes=g_scratch
        + [pltpu.VMEM((chans // 2, 2 * modes, 2 * nx), F32), pltpu.VMEM((chans, rows, nx), F32)],
        compiler_params=params,
        interpret=INTERPRET,
        name="middle",
    )(mixed, field_b, field_a, cot_a, uh, ul, th, tl, xh, xl, fh, fl, kron_f)

    back = scatter(back_part) * scale_i
    b_real, b_imag = back[0][None], back[1][None]
    grad_spec = gather(
        jnp.sum(b_real * w_real + b_imag * w_imag, axis=1) * scale_f,
        jnp.sum(b_imag * w_real - b_real * w_imag, axis=1) * scale_f,
    )
    grad_b = pl.pallas_call(
        lambda *refs: last_kernel(px, py, *refs),
        grid=(steps,),
        in_specs=[
            whole(part_shape.shape), block, block, u_block, u_block,
            whole(xh.shape), whole(xl.shape), whole((side, side)),
        ],
        out_specs=block,
        out_shape=field_shape,
        scratch_shapes=g_scratch + [pltpu.VMEM((chans, rows, nx), F32)],
        compiler_params=params,
        interpret=INTERPRET,
        name="last",
    )(grad_spec, slope, cot_b, uh, ul, xh, xl, kron_b)

    share = chans // samples
    spec_all = lax.all_gather(spectrum, "dp", axis=0)
    back_all = lax.all_gather(back, "dp", axis=0)
    back_own = lax.dynamic_slice_in_dim(back_all, lax.axis_index("dp") * share, share, axis=2)
    p_real, p_imag = spec_all[:, 0, :, None], spec_all[:, 1, :, None]
    q_real, q_imag = back_own[:, 0, None], back_own[:, 1, None]
    grad_real = jnp.sum(p_real * q_real + p_imag * q_imag, axis=0)
    grad_imag = jnp.sum(p_real * q_imag - p_imag * q_real, axis=0)
    grad = jnp.stack([grad_real, grad_imag]) * grad_scale
    spectral_grad = grad.reshape(2, chans, share, tall // MZ, MZ, kk).transpose(3, 4, 5, 0, 1, 2)

    point = jnp.sum(point.reshape(chans, SUB, chans, SUB) * jnp.eye(SUB, dtype=F32)[None, :, None, :], axis=(1, 3))
    point_total = lax.psum(point, ("dp", "px", "py")) * point_scale
    full = state_b.shape
    return (input_a.reshape(full), grad_b.reshape(full), spectral_grad, point_total)


def solution(mesh):
    return jax.shard_map(
        per_device,
        mesh=mesh,
        in_specs=(
            P("dp", None, "px", "py", None),
            P("dp", None, "px", "py", None),
            P("dp", None, "px", "py", None),
            P("dp", None, "px", "py", None),
            P("py", None, "px", None, None, None),
            P(),
        ),
        out_specs=(
            P("dp", None, "px", "py", None),
            P("dp", None, "px", "py", None),
            P("py", None, "px", None, None, "dp"),
            P(),
        ),
        check_vma=False,
    )
```

time: 1890 us -> 468 us (0.25)
  local copies, waits for them, and re-layouts: 798 us -> 26.7 us
  matrix products: 265 us -> 0 us
  blocking collectives: 312 us -> 54.9 us
  Pallas kernels: 0 us -> 161 us
  other arithmetic: 202 us -> 71.6 us
  waiting for transfers between devices: 255 us -> 139 us
  starting transfers between devices: 31.2 us -> 0.56 us
    all_to_all x21 -> x0, local copies, waits for them, and re-layouts: 354 us -> none  [the longest x6 158 us: inverse_field(): lax.all_to_all(along_y, 'px', split_axis=1, concat_axis=4, tiled=True)]
    unnamed x62 -> x4, local copies, waits for them, and re-layouts: 292 us -> 0.01 us
    dot_general x15 -> x0, matrix products: 265 us -> none  [the longest x2 89.1 us: inverse_field(): jnp.einsum('cyzrk,rkn->cyzn', lax.all_to_all(along_y, 'px', split_axis=1,...]
    all_to_all x5 -> x0, waiting for transfers between devices: 255 us -> none  [the longest x1 93.6 us: forward_field(): lax.all_to_all(along_x, 'px', split_axis=4, concat_axis=1, tiled=True)]
    all_to_all x3 -> x0, blocking collectives: 203 us -> none  [the longest x1 101 us: forward_field(): lax.all_to_all(along_x, 'px', split_axis=4, concat_axis=1, tiled=True)]
    all_to_all x8 -> x0, other arithmetic: 163 us -> none  [the longest x2 66.2 us: inverse_field(): lax.all_to_all(along_y, 'px', split_axis=1, concat_axis=4, tiled=True)]
    pallas_call x0 -> x3, Pallas kernels: none -> 161 us  [the longest x1 101 us: per_device(): pl.pallas_call(lambda *refs: middle_kernel(px, py, steps, *refs), grid=(s...]
    reduce_scatter x1 -> x2, waiting for transfers between devices: 0.01 us -> 105 us  [scatter(): lax.psum_scatter(value, ('px', 'py'), scatter_dimension=0, tiled=True)]
  transfers between devices with their start and end apart: 6 -> 4, of which waited for: 4 -> 3; matrix products, arithmetic and copies ran while one was open for 10% -> 9% of each run, Pallas kernels for 0% -> 0%
where the time goes in v1:
time: 468 us; the launch traced here: 467 us
  Pallas kernels  161 us (34%)
  waiting for transfers between devices  139 us (30%)
  other arithmetic  71.6 us (15%)
  blocking collectives  54.9 us (12%)
  local copies, waits for them, and re-layouts  26.7 us (6%)
  between operations  14.1 us (3%)
    reduce_scatter x2, waiting for transfers between devices, scatter(): lax.psum_scatter(value, ('px', 'py'), scatter_dimension=0, tiled=True)  105 us
    pallas_call x1, Pallas kernels, per_device(): pl.pallas_call(lambda *refs: middle_kernel(px, py, steps, *refs), grid=(s...  101 us
    pallas_call x1, Pallas kernels, per_device(): pl.pallas_call(lambda *refs: last_kernel(px, py, *refs), grid=(steps,), i...  42 us
    psum x1, blocking collectives, per_device(): point_total = lax.psum(point, ('dp', 'px', 'py')) * point_scale  39.6 us
    all_gather x2, waiting for transfers between devices, gather(): return lax.all_gather(value, ('px', 'py'), axis=0, tiled=True)  33.4 us
    pallas_call x1, Pallas kernels, per_device(): pl.pallas_call(lambda *refs: forward_kernel(px, py, *refs), grid=(groups,...  17.7 us
    mul x1, other arithmetic, per_device(): b_real * w_real + b_imag * w_imag  15.3 us
    reduce_sum x1, other arithmetic, per_device(): jnp.sum(s_real * w_real - s_imag * w_imag, axis=0) * scale_i  14.4 us
  transfers between devices with their start and end apart: 4, of which 3 were waited for; matrix products, arithmetic and copies ran while one was open for 9% of the time, Pallas kernels for 0%

profile of v1, /device:TPU:0, one launch (start us, length us, event | category | flops | bytes accessed | tf_op | source)
XLA Modules:
  0.0 467.3 jit_solution(5057968907816933059)
XLA Ops:
  7.6 1.1 fusion.11
  9.6 2.9 fusion.4
  12.4 17.7 %forward.1 = f32[8,4,64,128]{3,2,1,0:T(8,128)} custom-call(bf16[16,2048,128]{2,1,0:T(8,128)(2,1)} %bitcast.76, bf16[512,2048]{1,0:T(8,128)(2,1)} %get-tuple-element.25.refs_1_.refs_6_, bf16[512,2048]{1,0:T(8,128)(2,1)} %get-tuple-element.24.refs_2_.refs_7_, bf16[2,512,256]{2,1,0:T(8,128)(2,1)} %constant.151.clone.refs_3_.refs_10_, ...), custom_call_target="tpu_custom_call" | custom-call | tf_op jit(solution)/shard_map/forward/pallas_call | solution.py:264
  30.3 11.5 %convert_bitcast_fusion = f32[2,16,16,8,8,16]{2,1,0,5,4,3:T(8,128)} fusion(bf16[8,8,16,2,16,16]{5,4,3,2,1,0:T(8,128)(2,1)} %param.14), kind=kLoop, calls=%fused_computation | loop fusion | flops 524288 | bytes 3145728 | tf_op jit(solution)/shard_map/convert_element_type | solution.py:288
  41.9 11.4 %fusion.40 = (f32[1,16,16,8,8,16]{2,1,0,5,4,3:T(8,128)}, f32[1,16,16,8,8,16]{2,1,0,5,4,3:T(8,128)}) fusion(f32[2,16,16,8,8,16]{2,1,0,5,4,3:T(8,128)} %convert_bitcast_fusion), kind=kLoop, calls=%fused_computation.116 | loop fusion | bytes 4194304 | tf_op jit(solution)/shard_map/slice | solution.py:289
  53.2 43.2 %reduce-scatter.3.cloned.1.call-done = f32[1,4,64,128]{3,2,1,0:T(8,128)} async-done(((f32[8,4,64,128]{3,2,1,0:T(8,128)}), f32[1,4,64,128]{3,2,1,0:T(8,128)}) %reduce-scatter.3.cloned.1.call-update) | async-done | bytes 131088 | tf_op jit(solution)/shard_map/reduce_scatter | solution.py:279
  96.4 0.9 broadcast_multiply_fusion.3
  98.9 14.4 %fusion.1 = (f32[16,1024]{0,1:T(8,128)S(1)}, f32[16,1024]{0,1:T(8,128)S(1)}) fusion(f32[1,16,16,8,8,16]{2,1,0,5,4,3:T(8,128)} %get-tuple-element.17, f32[1,16,16,8,8,16]{2,1,0,5,4,3:T(8,128)} %get-tuple-element.16, f32[16,1024]{0,1:T(8,128)S(1)} %copy.88, f32[16,1024]{0,1:T(8,128)S(1)} %copy.86), kind=kLoop, calls=%fused_computation.6 | loop fusion | flops 2064384 | bytes 2359296 | tf_op jit(solution)/shard_map/reduce_sum | solution.py:293
  115.8 1.6 mul.601.refs_12_
  118.6 2.7 fusion.5
  121.3 33.4 %all-gather.3.cloned.1.call-done.refs_0_ = f32[8,4,64,128]{3,2,1,0:T(8,128)} async-done(((f32[1,4,64,128]{3,2,1,0:T(8,128)}), f32[8,4,64,128]{3,2,1,0:T(8,128)}) %all-gather.3.cloned.1.call-update) | async-done | bytes 1048592 | tf_op jit(solution)/shard_map/all_gather | solution.py:286
  154.7 100.9 %middle.1 = (bf16[16,2048,128]{2,1,0:T(8,128)(2,1)}, bf16[16,2048,128]{2,1,0:T(8,128)(2,1)}, f32[8,4,64,128]{3,2,1,0:T(8,128)}, f32[256,256]{1,0:T(8,128)}) custom-call(f32[8,4,64,128]{3,2,1,0:T(8,128)} %all-gather.3.cloned.1.call-done.refs_0_, bf16[16,2048,128]{2,1,0:T(8,128)(2,1)} %bitcast.77, bf16[16,2048,128]{2,1,0:T(8,128)(2,1)} %bitcast.82, ...), custom_call_target="tpu_custom_call" | custom-call | tf_op jit(solution)/shard_map/middle/pallas_call | solution.py:305
  255.9 62.1 %reduce-scatter.5.cloned.1.call-done = f32[1,4,64,128]{3,2,1,0:T(8,128)} async-done(((f32[8,4,64,128]{3,2,1,0:T(8,128)}), f32[1,4,64,128]{3,2,1,0:T(8,128)}) %reduce-scatter.5.cloned.1.call-update) | async-done | bytes 131088 | tf_op jit(solution)/shard_map/reduce_scatter | solution.py:279
  318.0 0.9 broadcast_multiply_fusion.2
  320.4 15.3 %bitcast_multiply_fusion.5 = (f32[16,16,1024]{1,0,2:T(8,128)}, f32[16,16,1024]{1,0,2:T(8,128)}, f32[16,16,1024]{1,0,2:T(8,128)}, f32[16,16,1024]{1,0,2:T(8,128)}) fusion(f32[1,16,16,8,8,16]{2,1,0,5,4,3:T(8,128)} %get-tuple-element.16, f32[16,1024]{0,1:T(8,128)S(1)} %copy.98, f32[16,1024]{0,1:T(8,128)S(1)} %copy.100, ...), kind=kLoop, calls=%fused_computation.10 | loop fusion | flops 1048576 | bytes 6422528 | tf_op jit(solution)/shard_map/mul | solution.py:324
  335.7 13.1 %subtract_reduce_fusion = (f32[16,1024]{0,1:T(8,128)S(1)}, f32[16,1024]{0,1:T(8,128)S(1)}) fusion(f32[16,16,1024]{1,0,2:T(8,128)} %get-tuple-element.21, f32[16,16,1024]{1,0,2:T(8,128)} %get-tuple-element.26, f32[16,16,1024]{1,0,2:T(8,128)} %get-tuple-element.20, f32[16,16,1024]{1,0,2:T(8,128)} %get-tuple-element.27), kind=kLoop, calls=%fused_computation.13 | loop fusion | flops 1015808 | bytes 4325376 | tf_op jit(solution)/shard_map/reduce_sum | solution.py:325
  350.8 1.6 mul.620.refs_7_
  353.4 7.1 %all_gather.16 = f32[4,2,16,1024]{3,2,1,0:T(8,128)S(1)} all-gather(f32[1,2,16,1024]{3,2,1,0:T(8,128)S(1)} %mul.621), channel_id=1, replica_groups=mesh['dp'=4,'px'=2,'py'=4] {'dp'}, dimensions={0}, use_global_device_ids=true | all-gather | bytes 655360 | tf_op jit(solution)/shard_map/all_gather | solution.py:343
  361.5 39.6 %psum.7 = f32[16,16]{1,0:T(8,128)S(1)} all-reduce(f32[16,16]{1,0:T(8,128)S(1)} %multiply_reduce_fusion), channel_id=1, replica_groups=mesh['dp'=4,'px'=2,'py'=4] {'dp','px','py'}, use_global_device_ids=true, to_apply=%region_9.10 | all-reduce | flops 256 | bytes 2048 | tf_op jit(solution)/shard_map/psum | solution.py:354
  402.7 8.2 %all_gather.17 = f32[4,2,16,1024]{3,2,1,0:T(8,128)S(1)} all-gather(f32[1,2,16,1024]{3,2,1,0:T(8,128)S(1)} %mul.624), channel_id=1, replica_groups=mesh['dp'=4,'px'=2,'py'=4] {'dp'}, dimensions={0}, use_global_device_ids=true | all-gather | bytes 655360 | tf_op jit(solution)/shard_map/all_gather | solution.py:344
  411.2 0.8 copy.112
  412.1 1.7 copy.111
  413.8 5.0 %fusion.6 = f32[8,8,16,2,16,4]{4,5,3,2,1,0:T(4,128)} fusion(f32[1,16,4,8,8,16]{1,2,0,5,4,3:T(4,128)S(1)} %bitcast.80, f32[1,16,4,8,8,16]{1,2,0,5,4,3:T(4,128)} %bitcast.81), kind=kLoop, calls=%fused_computation.24 | loop fusion | flops 262144 | bytes 1048576 | tf_op jit(solution)/shard_map/transpose | solution.py:351
  418.8 42.0 %last.1 = bf16[16,2048,128]{2,1,0:T(8,128)(2,1)} custom-call(f32[8,4,64,128]{3,2,1,0:T(8,128)} %all-gather.5.cloned.1.call-done.refs_0_, bf16[16,2048,128]{2,1,0:T(8,128)(2,1)} %get-tuple-element.10.refs_1_, bf16[16,2048,128]{2,1,0:T(8,128)(2,1)} %bitcast.84, bf16[2048,512]{1,0:T(8,128)(2,1)} %get-tuple-element.23.refs_4_.refs_3_, ...), custom_call_target="tpu_custom_call" | custom-call | tf_op jit(solution)/shard_map/last/pallas_call | solution.py:327
  (79 shorter events, 14.0 us)
Async XLA Ops:
  7.2 89.3 %reduce-scatter.3.cloned.1.call-start = ((), (), s32[]{:S(2)}) async-start(), calls=%async_computation.2 | async-start | bytes 1179648 | tf_op jit(solution)/shard_map/reduce_scatter | solution.py:279
  12.4 17.8 %copy-start.1 = (bf16[16,16]{1,0:T(8,128)(2,1)S(1)}, bf16[16,16]{1,0:T(8,128)(2,1)}, u32[]{:S(2)}) copy-start(bf16[16,16]{1,0:T(8,128)(2,1)} %param.15) | copy-start | bytes 1540
  30.2 124.5 %all-gather.3.cloned.1.call-start = ((), (), s32[]{:S(2)}) async-start(), calls=%async_computation.3 | async-start | bytes 1179648 | tf_op jit(solution)/shard_map/all_gather | solution.py:286
  115.3 202.6 %reduce-scatter.5.cloned.1.call-start = ((), (), s32[]{:S(2)}) async-start(), calls=%async_computation.4 | async-start | bytes 1179648 | tf_op jit(solution)/shard_map/reduce_scatter | solution.py:279
  255.6 163.2 %all-gather.5.cloned.1.call-start = ((), (), s32[]{:S(2)}) async-start(), calls=%async_computation.5 | async-start | bytes 1179648 | tf_op jit(solution)/shard_map/all_gather | solution.py:286
  349.5 11.1 %copy-start = (f32[256,256]{1,0:T(8,128)S(1)}, f32[256,256]{1,0:T(8,128)}, u32[]{:S(2)}) copy-start(f32[256,256]{1,0:T(8,128)} %get-tuple-element.11) | copy-start | bytes 786436
Sparse Core Ops, SparseCore 0:
  30.3 66.0 reduce-scatter.2
  115.4 39.2 all-gather.2
  255.7 62.1 reduce-scatter.4
  350.9 39.0 all-gather.4

commit v2 on v1

--- a/solution.py
+++ b/solution.py
@@ -25,11 +25,6 @@
 
 def angle(product, length_all):
     return (product % length_all).astype(F32) * (2.0 * math.pi / length_all)
-
-
-def split(value):
-    high = lax.reduce_precision(value, 8, 7)
-    return high.astype(BF16), (value - high).astype(BF16)
 
 
 def synthesis_table(shape):
@@ -105,7 +100,7 @@
             out_ref[i * py + j, group] = value[j * tall : (j + 1) * tall, i * wide : (i + 1) * wide]
 
 
-def build_fields(spec_ref, xh_ref, xl_ref, gh_ref, gl_ref, px, py):
+def build_fields(spec_ref, xh_ref, xl_ref, gh_ref, px, py):
     modes = MY * MZ
     for g in range(spec_ref.shape[1]):
         rows = []
@@ -113,11 +108,10 @@
             rows.append(jnp.concatenate([spec_ref[i * py + j, g] for i in range(px)], axis=1))
         value = jnp.concatenate(rows, axis=0)
         for t in range(2):
-            high, low = cut(dot3(value, xh_ref[t], xl_ref[t]))
+            high = dot3(value, xh_ref[t], xl_ref[t]).astype(BF16)
             half = high.shape[1] // 2
             for h in range(2):
                 gh_ref[2 * g + h, t * modes : (t + 1) * modes] = high[:, h * half : (h + 1) * half]
-                gl_ref[2 * g + h, t * modes : (t + 1) * modes] = low[:, h * half : (h + 1) * half]
 
 
 def pair_of(ref, start):
@@ -140,20 +134,119 @@
     lax.fori_loop(0, rows // (2 * SUB), body, 0)
 
 
-def forward_kernel(px, py, v_ref, th_ref, tl_ref, xh_ref, xl_ref, out_ref):
+def position(py):
+    return lax.axis_index("px") * py + lax.axis_index("py")
+
+
+def partner(px, py, offset):
+    other = lax.rem(position(py) + offset, px * py)
+    return other, {"px": lax.div(other, py), "py": lax.rem(other, py)}
+
+
+def greet(px, py):
+    barrier = pltpu.get_barrier_semaphore()
+    for offset in range(1, px * py):
+        pl.semaphore_signal(
+            barrier, inc=1, device_id=partner(px, py, offset)[1], device_id_type=pl.DeviceIdType.MESH
+        )
+    pl.semaphore_wait(barrier, px * py - 1)
+
+
+def scatter_copy(px, py, offset, group, part_ref, land_ref, send_sem, recv_sem):
+    other, device = partner(px, py, offset)
+    return pltpu.make_async_remote_copy(
+        part_ref.at[other, group], land_ref.at[offset, group], send_sem.at[offset, group], recv_sem.at[offset, group],
+        device_id=device, device_id_type=pl.DeviceIdType.MESH,
+    )
+
+
+def scatter_kernel(px, py, part_ref, out_ref, land_ref, send_sem, recv_sem):
+    count = px * py
+    greet(px, py)
+    groups = part_ref.shape[1]
+    for g in range(groups):
+        for offset in range(1, count):
+            scatter_copy(px, py, offset, g, part_ref, land_ref, send_sem, recv_sem).start()
+    out_ref[...] = part_ref[position(py)]
+    for g in range(groups):
+        for offset in range(1, count):
+            scatter_copy(px, py, offset, g, part_ref, land_ref, send_sem, recv_sem).wait()
+            out_ref[g] += land_ref[offset, g]
+
+
+def gather_kernel(px, py, own_ref, out_ref, land_ref, send_sem, recv_sem):
+    count = px * py
+    greet(px, py)
+    copies = []
+    for offset in range(1, count):
+        copies.append(
+            pltpu.make_async_remote_copy(
+                own_ref, land_ref.at[offset], send_sem.at[offset], recv_sem.at[offset],
+                device_id=partner(px, py, offset)[1], device_id_type=pl.DeviceIdType.MESH,
+            )
+        )
+        copies[-1].start()
+    here = position(py)
+    out_ref[here] = own_ref[...]
+    for offset in range(1, count):
+        copies[offset - 1].wait()
+        out_ref[lax.rem(here + count - offset, count)] = land_ref[offset]
+
+
+def mix_kernel(s_ref, w_ref, out_ref):
+    chans = s_ref.shape[1]
+    real = jnp.zeros(out_ref.shape[1:], F32)
+    imag = jnp.zeros(out_ref.shape[1:], F32)
+    for c in range(chans):
+        s_real, s_imag = s_ref[0, c : c + 1], s_ref[1, c : c + 1]
+        w_real, w_imag = w_ref[0, c].astype(F32), w_ref[1, c].astype(F32)
+        real += s_real * w_real - s_imag * w_imag
+        imag += s_real * w_imag + s_imag * w_real
+    out_ref[0] = real
+    out_ref[1] = imag
+
+
+def adjoint_kernel(b_ref, w_ref, out_ref):
+    b_real, b_imag = b_ref[0], b_ref[1]
+    for c in range(w_ref.shape[1]):
+        w_real, w_imag = w_ref[0, c].astype(F32), w_ref[1, c].astype(F32)
+        out_ref[0, c : c + 1] = jnp.sum(b_real * w_real + b_imag * w_imag, axis=0, keepdims=True)
+        out_ref[1, c : c + 1] = jnp.sum(b_imag * w_real - b_real * w_imag, axis=0, keepdims=True)
+
+
+def forward_kernel(
+    px, py, v_ref, th_ref, xh_ref, xl_ref, out_ref, part_ref, land_ref, send_sem, recv_sem
+):
     modes = MY * MZ
     parts = []
     for p in range(GROUP // 2):
         value = jnp.concatenate([v_ref[2 * p], v_ref[2 * p + 1]], axis=1)
-        parts.append(dot(th_ref[...], value) + dot(tl_ref[...], value))
+        parts.append(dot(th_ref[...], value))
     b0 = jnp.concatenate([part[:modes] for part in parts], axis=1)
     b1 = jnp.concatenate([part[modes:] for part in parts], axis=1)
-    store_modes(out_ref, 0, to_modes(b0, b1, xh_ref, xl_ref), px, py)
+    step = pl.program_id(0)
+    store_modes(part_ref, step, to_modes(b0, b1, xh_ref, xl_ref), px, py)
+    count = px * py
+
+    @pl.when(step == 0)
+    def _():
+        greet(px, py)
+
+    for offset in range(1, count):
+        scatter_copy(px, py, offset, step, part_ref, land_ref, send_sem, recv_sem).start()
+
+    @pl.when(step == pl.num_programs(0) - 1)
+    def _():
+        out_ref[...] = part_ref[position(py)]
+        for g in range(part_ref.shape[1]):
+            for offset in range(1, count):
+                scatter_copy(px, py, offset, g, part_ref, land_ref, send_sem, recv_sem).wait()
+                out_ref[g] += land_ref[offset, g]
 
 
 def middle_kernel(
-    px, py, steps, spec_ref, vb_ref, va_ref, ca_ref, uh_ref, ul_ref, th_ref, tl_ref, xh_ref, xl_ref, fh_ref, fl_ref,
-    kron_ref, ia_ref, sl_ref, back_ref, point_ref, gh_ref, gl_ref, acc_ref, mix_ref,
+    px, py, steps, spec_ref, vb_ref, va_ref, ca_ref, uh_ref, th_ref, xh_ref, xl_ref, fh_ref, fl_ref,
+    kron_ref, ia_ref, sl_ref, back_ref, point_ref, gh_ref, acc_ref, mix_ref,
 ):
     step = pl.program_id(0)
     modes = MY * MZ
@@ -162,7 +255,7 @@
 
     @pl.when(step == 0)
     def _():
-        build_fields(spec_ref, xh_ref, xl_ref, gh_ref, gl_ref, px, py)
+        build_fields(spec_ref, xh_ref, xl_ref, gh_ref, px, py)
         acc_ref[...] = jnp.zeros_like(acc_ref)
         point_ref[...] = jnp.zeros_like(point_ref)
 
@@ -170,7 +263,7 @@
     c0 = math.sqrt(2.0 / math.pi)
 
     def body(p, carry):
-        field = dot(uh_ref[...], gh_ref[p]) + dot(ul_ref[...], gh_ref[p]) + dot(uh_ref[...], gl_ref[p])
+        field = dot(uh_ref[...], gh_ref[p])
         slopes = []
         for h in range(2):
             d = 2 * p + h
@@ -184,7 +277,7 @@
             sl_ref[d] = slope
             slopes.append(slope)
         both = jnp.concatenate(slopes, axis=1)
-        acc_ref[p] += dot(th_ref[...], both) + dot(tl_ref[...], both)
+        acc_ref[p] += dot(th_ref[...], both)
         return carry
 
     lax.fori_loop(0, chans // 2, body, 0)
@@ -208,18 +301,18 @@
 
 
 def last_kernel(
-    px, py, spec_ref, sl_ref, cb_ref, uh_ref, ul_ref, xh_ref, xl_ref, kron_ref, out_ref, gh_ref, gl_ref, mix_ref
+    px, py, spec_ref, sl_ref, cb_ref, uh_ref, xh_ref, xl_ref, kron_ref, out_ref, gh_ref, mix_ref
 ):
     nx = sl_ref.shape[2]
 
     @pl.when(pl.program_id(0) == 0)
     def _():
-        build_fields(spec_ref, xh_ref, xl_ref, gh_ref, gl_ref, px, py)
+        build_fields(spec_ref, xh_ref, xl_ref, gh_ref, px, py)
 
     channel_mix(kron_ref, sl_ref, mix_ref)
 
     def body(p, carry):
-        field = dot(uh_ref[...], gh_ref[p]) + dot(ul_ref[...], gh_ref[p]) + dot(uh_ref[...], gl_ref[p])
+        field = dot(uh_ref[...], gh_ref[p])
         for h in range(2):
             d = 2 * p + h
             value = cb_ref[d].astype(F32) + field[:, h * nx : (h + 1) * nx] + mix_ref[d]
@@ -247,8 +340,8 @@
     grad_scale = math.sqrt(MX * MY * MZ / (samples * nx * ny * nz))
     point_scale = 1.0 / math.sqrt(samples * nx * ny * nz)
     shape = (ys, zs, ny, nz)
-    th, tl = split(analysis_table(shape))
-    uh, ul = split(synthesis_table(shape))
+    th = analysis_table(shape).astype(BF16)
+    uh = synthesis_table(shape).astype(BF16)
     xh, xl = x_tables(px, nx)
     fh, fl = (jnp.asarray(np.ascontiguousarray(table.transpose(0, 2, 1))) for table in (xh, xl))
     xh, xl = jnp.asarray(xh), jnp.asarray(xl)
@@ -261,38 +354,63 @@
     part_shape = jax.ShapeDtypeStruct((px * py, groups, tall, wide), F32)
     params = pltpu.CompilerParams(vmem_limit_bytes=LIMIT)
 
-    part = pl.pallas_call(
+    count = px * py
+    own_shape = jax.ShapeDtypeStruct((groups, tall, wide), F32)
+    exchange = [
+        pltpu.VMEM(part_shape.shape, F32),
+        pltpu.SemaphoreType.DMA((count, groups)),
+        pltpu.SemaphoreType.DMA((count, groups)),
+    ]
+
+    def linked(number):
+        return pltpu.CompilerParams(vmem_limit_bytes=LIMIT, collective_id=number, has_side_effects=True)
+
+    def to_channels(value):
+        value = value.reshape(groups, tall, GROUP, 2, kk).transpose(3, 0, 2, 1, 4)
+        return value.reshape(2, chans, own)
+
+    def gather(value, number):
+        value = value.reshape(2, groups, GROUP, tall, kk).transpose(1, 3, 2, 0, 4)
+        value = value.reshape(groups, tall, wide)
+        return pl.pallas_call(
+            lambda *refs: gather_kernel(px, py, *refs),
+            in_specs=[pl.BlockSpec(memory_space=pltpu.VMEM)],
+            out_specs=pl.BlockSpec(memory_space=pltpu.VMEM),
+            out_shape=part_shape,
+            scratch_shapes=[
+                pltpu.VMEM(part_shape.shape, F32), pltpu.SemaphoreType.DMA((count,)), pltpu.SemaphoreType.DMA((count,)),
+            ],
+            compiler_params=linked(number),
+            interpret=INTERPRET,
+            name="gather",
+        )(value)
+
+    def mode_product(kernel, value, name):
+        return pl.pallas_call(
+            kernel,
+            out_shape=jax.ShapeDtypeStruct((2, chans, own), F32),
+            compiler_params=params,
+            interpret=INTERPRET,
+            name=name,
+        )(value, weight)
+
+    spectrum = pl.pallas_call(
         lambda *refs: forward_kernel(px, py, *refs),
         grid=(groups,),
         in_specs=[
             pl.BlockSpec((GROUP, cells, nx), lambda i: (i, 0, 0)),
-            whole(th.shape), whole(tl.shape), whole(fh.shape), whole(fl.shape),
+            whole(th.shape), whole(fh.shape), whole(fl.shape),
         ],
-        out_specs=pl.BlockSpec((px * py, 1, tall, wide), lambda i: (0, i, 0, 0)),
-        out_shape=part_shape,
-        compiler_params=params,
+        out_specs=whole(own_shape.shape),
+        out_shape=own_shape,
+        scratch_shapes=[pltpu.VMEM(part_shape.shape, F32)] + exchange,
+        compiler_params=linked(0),
         interpret=INTERPRET,
         name="forward",
-    )(field_b, th, tl, fh, fl)
-
-    def scatter(value):
-        value = lax.psum_scatter(value, ("px", "py"), scatter_dimension=0, tiled=True)
-        value = value.reshape(groups, tall, GROUP, 2, kk).transpose(3, 0, 2, 1, 4)
-        return value.reshape(2, chans, own)
-
-    def gather(real, imag):
-        value = jnp.stack([real, imag]).reshape(2, groups, GROUP, tall, kk).transpose(1, 3, 2, 0, 4)
-        value = value.reshape(1, groups, tall, wide)
-        return lax.all_gather(value, ("px", "py"), axis=0, tiled=True)
-
-    weight = spectral_weight.transpose(3, 4, 5, 0, 1, 2).reshape(2, chans, chans, own).astype(F32)
-    w_real, w_imag = weight[0], weight[1]
-    spectrum = scatter(part) * scale_f
-    s_real, s_imag = spectrum[0][:, None], spectrum[1][:, None]
-    mixed = gather(
-        jnp.sum(s_real * w_real - s_imag * w_imag, axis=0) * scale_i,
-        jnp.sum(s_real * w_imag + s_imag * w_real, axis=0) * scale_i,
-    )
+    )(field_b, th, fh, fl)
+    weight = spectral_weight.transpose(3, 4, 5, 0, 1, 2).reshape(2, chans, chans, own)
+    spectrum = to_channels(spectrum) * scale_f
+    mixed = gather(mode_product(mix_kernel, spectrum, "mix") * scale_i, 1)
 
     rows = min(256, cells)
     steps = cells // rows
@@ -301,12 +419,12 @@
     t_block = pl.BlockSpec((2 * modes, rows), lambda i: (0, i))
     field_shape = jax.ShapeDtypeStruct((chans, cells, nx), BF16)
     side = chans * SUB
-    g_scratch = [pltpu.VMEM((chans // 2, 2 * modes, 2 * nx), BF16)] * 2
+    g_scratch = [pltpu.VMEM((chans // 2, 2 * modes, 2 * nx), BF16)]
     input_a, slope, back_part, point = pl.pallas_call(
         lambda *refs: middle_kernel(px, py, steps, *refs),
         grid=(steps,),
         in_specs=[
-            whole(part_shape.shape), block, block, block, u_block, u_block, t_block, t_block,
+            whole(part_shape.shape), block, block, block, u_block, t_block,
             whole(xh.shape), whole(xl.shape), whole(fh.shape), whole(fl.shape), whole((side, side)),
         ],
         out_specs=[block, block, whole(part_shape.shape), whole((side, side))],
@@ -316,19 +434,25 @@
         compiler_params=params,
         interpret=INTERPRET,
         name="middle",
-    )(mixed, field_b, field_a, cot_a, uh, ul, th, tl, xh, xl, fh, fl, kron_f)
-
-    back = scatter(back_part) * scale_i
-    b_real, b_imag = back[0][None], back[1][None]
-    grad_spec = gather(
-        jnp.sum(b_real * w_real + b_imag * w_imag, axis=1) * scale_f,
-        jnp.sum(b_imag * w_real - b_real * w_imag, axis=1) * scale_f,
-    )
+    )(mixed, field_b, field_a, cot_a, uh, th, xh, xl, fh, fl, kron_f)
+
+    back = pl.pallas_call(
+        lambda *refs: scatter_kernel(px, py, *refs),
+        in_specs=[pl.BlockSpec(memory_space=pltpu.VMEM)],
+        out_specs=pl.BlockSpec(memory_space=pltpu.VMEM),
+        out_shape=own_shape,
+        scratch_shapes=exchange,
+        compiler_params=linked(2),
+        interpret=INTERPRET,
+        name="scatter",
+    )(back_part)
+    back = to_channels(back) * scale_i
+    grad_spec = gather(mode_product(adjoint_kernel, back, "adjoint") * scale_f, 3)
     grad_b = pl.pallas_call(
         lambda *refs: last_kernel(px, py, *refs),
         grid=(steps,),
         in_specs=[
-            whole(part_shape.shape), block, block, u_block, u_block,
+            whole(part_shape.shape), block, block, u_block,
             whole(xh.shape), whole(xl.shape), whole((side, side)),
         ],
         out_specs=block,
@@ -337,7 +461,7 @@
         compiler_params=params,
         interpret=INTERPRET,
         name="last",
-    )(grad_spec, slope, cot_b, uh, ul, xh, xl, kron_b)
+    )(grad_spec, slope, cot_b, uh, xh, xl, kron_b)
 
     share = chans // samples
     spec_all = lax.all_gather(spectrum, "dp", axis=0)

time: 468 us -> 334 us (0.71)
  waiting for transfers between devices: 139 us -> 0 us
  Pallas kernels: 161 us -> 237 us
  other arithmetic: 71.6 us -> 16.6 us
  between operations: 14.1 us -> 0.88 us
    reduce_scatter x2 -> x0, waiting for transfers between devices: 105 us -> none  [scatter(): lax.psum_scatter(value, ('px', 'py'), scatter_dimension=0, tiled=True)]
    pallas_call x0 -> x5, Pallas kernels: none -> 90.1 us  [the longest x2 53.9 us: gather(): pl.pallas_call(lambda *refs: gather_kernel(px, py, *refs), in_specs=[pl.B...]
    all_gather x2 -> x0, waiting for transfers between devices: 33.4 us -> none  [gather(): return lax.all_gather(value, ('px', 'py'), axis=0, tiled=True)]
    reduce_sum x2 -> x0, other arithmetic: 27.4 us -> none  [the longest x1 14.4 us: per_device(): jnp.sum(s_real * w_real - s_imag * w_imag, axis=0) * scale_i]
    pallas_call x1, Pallas kernels: 101 us -> 78.4 us  [per_device(): pl.pallas_call(lambda *refs: middle_kernel(px, py, steps, *refs), grid=(s...]
    pallas_call x1, Pallas kernels: 17.7 us -> 35.2 us  [per_device(): pl.pallas_call(lambda *refs: forward_kernel(px, py, *refs), grid=(groups,...]
    convert_element_type x3 -> x0, other arithmetic: 17.1 us -> none  [the longest x1 11.5 us: per_device(): spectral_weight.transpose(3, 4, 5, 0, 1, 2).reshape(2, chans, chans, own)]
    mul x7 -> x4, other arithmetic: 17.2 us -> 3.67 us  [the longest x1 0.92 us: per_device(): spectrum = to_channels(spectrum) * scale_f]
  transfers between devices with their start and end apart: 4 -> 0, of which waited for: 3 -> 0; matrix products, arithmetic and copies ran while one was open for 9% -> 0% of each run, Pallas kernels for 0% -> 0%
where the time goes in v2:
time: 334 us; the launch traced here: 333 us
  Pallas kernels  237 us (71%)
  blocking collectives  55.2 us (17%)
  local copies, waits for them, and re-layouts  24.2 us (7%)
  other arithmetic  16.6 us (5%)
    pallas_call x1, Pallas kernels, per_device(): pl.pallas_call(lambda *refs: middle_kernel(px, py, steps, *refs), grid=(s...  78.4 us
    pallas_call x2, Pallas kernels, gather(): pl.pallas_call(lambda *refs: gather_kernel(px, py, *refs), in_specs=[pl.B...  53.9 us
    psum x1, blocking collectives, per_device(): point_total = lax.psum(point, ('dp', 'px', 'py')) * point_scale  41.1 us
    pallas_call x1, Pallas kernels, per_device(): pl.pallas_call(lambda *refs: forward_kernel(px, py, *refs), grid=(groups,...  35.2 us
    pallas_call x1, Pallas kernels, per_device(): pl.pallas_call(lambda *refs: last_kernel(px, py, *refs), grid=(steps,), i...  33 us
    pallas_call x1, Pallas kernels, per_device(): pl.pallas_call(lambda *refs: scatter_kernel(px, py, *refs), in_specs=[pl....  31.2 us
    reshape x1, local copies, waits for them, and re-layouts, per_device(): spectral_weight.transpose(3, 4, 5, 0, 1, 2).reshape(2, chans, chans, own)  9.11 us
    all_gather x1, blocking collectives, per_device(): spec_all = lax.all_gather(spectrum, 'dp', axis=0)  7.38 us

profile of v2, /device:TPU:0, one launch (start us, length us, event | category | flops | bytes accessed | tf_op | source)
XLA Modules:
  0.0 333.5 jit_solution(11836228266810550398)
XLA Ops:
  2.4 1.1 fusion.5
  3.5 9.1 %copy.58.w_ref = bf16[2,16,16,1024]{3,2,1,0:T(8,128)(2,1)} copy(bf16[2,16,16,1024]{2,1,0,3:T(8,128)(2,1)} %bitcast.53) | data formatting | bytes 2097152 | tf_op jit(solution)/shard_map/reshape | solution.py:411
  13.2 1.5 pad_maximum_fusion
  14.7 35.2 %forward.1 = f32[4,64,128]{2,1,0:T(8,128)} custom-call(bf16[16,2048,128]{2,1,0:T(8,128)(2,1)} %bitcast.47, bf16[512,2048]{1,0:T(8,128)(2,1)} %bitcast.49, bf16[2,512,256]{2,1,0:T(8,128)(2,1)} %constant.149.clone.refs_2_.refs_8_, bf16[2,512,256]{2,1,0:T(8,128)(2,1)} %constant.150.clone.refs_3_.refs_9_), custom_call_target="tpu_custom_call" | custom-call | tf_op jit(solution)/shard_map/forward/pallas_call | solution.py:397
  49.8 0.9 broadcast_multiply_fusion.5
  51.9 1.3 mul.425.s_ref
  53.2 2.4 mix.1
  56.5 7.4 %all_gather.8 = f32[4,2,16,1024]{3,2,1,0:T(8,128)S(1)} all-gather(f32[1,2,16,1024]{3,2,1,0:T(8,128)S(1)} %mul.457), channel_id=1, replica_groups=mesh['dp'=4,'px'=2,'py'=4] {'dp'}, dimensions={0}, use_global_device_ids=true | all-gather | bytes 655360 | tf_op jit(solution)/shard_map/all_gather | solution.py:467
  65.4 26.9 %gather.2.refs_0_ = f32[8,4,64,128]{3,2,1,0:T(8,128)} custom-call(f32[4,64,128]{2,1,0:T(8,128)} %copy.48.refs_0_), custom_call_target="tpu_custom_call" | custom-call | tf_op jit(solution)/shard_map/gather/pallas_call | solution.py:375
  92.3 0.9 subtract_convert_fusion
  93.3 1.5 pad_maximum_fusion.1.refs_4_.refs_3_
  95.0 1.6 mul.456.refs_6_
  96.7 1.6 mul.448.refs_10_
  98.3 78.4 %middle.1 = (bf16[16,2048,128]{2,1,0:T(8,128)(2,1)}, bf16[16,2048,128]{2,1,0:T(8,128)(2,1)}, f32[8,4,64,128]{3,2,1,0:T(8,128)}, f32[256,256]{1,0:T(8,128)}) custom-call(f32[8,4,64,128]{3,2,1,0:T(8,128)} %gather.2.refs_0_, bf16[16,2048,128]{2,1,0:T(8,128)(2,1)} %bitcast.48, bf16[16,2048,128]{2,1,0:T(8,128)(2,1)} %bitcast.56, bf16[16,2048,128]{2,1,0:T(8,128)(2,1)} %bitcast.57, ...), custom_call_target="tpu_custom_call" | custom-call | tf_op jit(solution)/shard_map/middle/pallas_call | solution.py:423
  176.7 31.2 %scatter.1 = f32[4,64,128]{2,1,0:T(8,128)} custom-call(f32[8,4,64,128]{3,2,1,0:T(8,128)} %get-tuple-element.9.refs_0_), custom_call_target="tpu_custom_call" | custom-call | tf_op jit(solution)/shard_map/scatter/pallas_call | solution.py:439
  207.9 0.9 broadcast_multiply_fusion.3
  210.0 1.3 mul.452.b_ref
  211.3 2.6 adjoint.1
  214.8 6.7 %all_gather.9 = f32[4,2,16,1024]{3,2,1,0:T(8,128)S(1)} all-gather(f32[1,2,16,1024]{3,2,1,0:T(8,128)S(1)} %mul.460), channel_id=1, replica_groups=mesh['dp'=4,'px'=2,'py'=4] {'dp'}, dimensions={0}, use_global_device_ids=true | all-gather | bytes 655360 | tf_op jit(solution)/shard_map/all_gather | solution.py:468
  223.3 26.9 %gather.3.refs_0_ = f32[8,4,64,128]{3,2,1,0:T(8,128)} custom-call(f32[4,64,128]{2,1,0:T(8,128)} %copy.53.refs_0_), custom_call_target="tpu_custom_call" | custom-call | tf_op jit(solution)/shard_map/gather/pallas_call | solution.py:375
  250.2 33.0 %last.1 = bf16[16,2048,128]{2,1,0:T(8,128)(2,1)} custom-call(f32[8,4,64,128]{3,2,1,0:T(8,128)} %gather.3.refs_0_, bf16[16,2048,128]{2,1,0:T(8,128)(2,1)} %get-tuple-element.10.refs_1_, bf16[16,2048,128]{2,1,0:T(8,128)(2,1)} %bitcast.51, bf16[2048,512]{1,0:T(8,128)(2,1)} %pad_maximum_fusion.1.refs_4_.refs_3_, ...), custom_call_target="tpu_custom_call" | custom-call | tf_op jit(solution)/shard_map/last/pallas_call | solution.py:451
  284.1 1.8 copy.60
  285.8 5.0 %fusion = f32[8,8,16,2,16,4]{4,5,3,2,1,0:T(4,128)} fusion(f32[1,16,4,8,8,16]{1,2,0,5,4,3:T(4,128)} %bitcast.55, f32[1,16,4,8,8,16]{1,2,0,5,4,3:T(4,128)S(1)} %bitcast.54), kind=kLoop, calls=%fused_computation.1 | loop fusion | flops 262144 | bytes 1048576 | tf_op jit(solution)/shard_map/transpose | solution.py:475
  291.8 41.1 %psum.7 = f32[16,16]{1,0:T(8,128)S(1)} all-reduce(f32[16,16]{1,0:T(8,128)S(1)} %multiply_reduce_fusion), channel_id=1, replica_groups=mesh['dp'=4,'px'=2,'py'=4] {'dp','px','py'}, use_global_device_ids=true, to_apply=%region_3.4 | all-reduce | flops 256 | bytes 2048 | tf_op jit(solution)/shard_map/psum | solution.py:478
  (41 shorter events, 12.1 us)
Async XLA Ops:
  93.3 1.6 copy-start.1
  285.8 5.0 %copy-start = (f32[256,256]{1,0:T(8,128)S(1)}, f32[256,256]{1,0:T(8,128)}, u32[]{:S(2)}) copy-start(f32[256,256]{1,0:T(8,128)} %get-tuple-element.11) | copy-start | bytes 786436
